TPU v7x, 512 devices: a whole 4x8x8 slice. The times are simulated.
512 devices in a mesh: scen: 8 (over y), blk: 64 (over z, x, core).
Axes of the slice: x: 4, y: 8, z: 8, core: 2. Of those that a mesh axis runs over, the one named last changes fastest.
Arguments:
- returns: bfloat16 [512, 32768], P(('scen', 'blk')), may hold values from -6 to 6
- vol_hist: float32 [512, 32768], P(('scen', 'blk')), may hold values from 0.5 to 5.5, as said below
- vol_now: float32 [32768], replicated, may hold values from 0.5 to 2
- sensitivity: bfloat16 [16384, 128, 128], P('blk'), may hold values from -0.109375 to 0.109375
- block_pairs: int32 [16384, 3], P('blk'), may hold values from 0 to 255, as said below
- book_order: int32 [128], replicated, may hold values from 0 to 127, each once
Outputs:
- profit_loss: float32 [512, 16384], P('scen', 'blk')
- book_rms: float32 [16384], P('blk')
Inputs may be any that keep to these rules, and one draw needn't show every extreme that they name: `block_pairs`: each index k of blk holds 256 slots; their factor blocks lie in k * 4 to k * 4 + 3; on each index the live slots come first; some index has all 256 slots live. `vol_hist`: positive volatilities.
All inputs are finite; a program needn't handle non-finite values.
Results may differ from a plain program's by a relative error of at most 0.0029.
Values may be sent and summed in bfloat16 or wider, within the bound.
A program may use at most 64 MiB of HBM per device.

v0:
```python
import jax
import jax.numpy as jnp
from jax import lax
from jax.sharding import PartitionSpec as P


def shards(returns, vol_hist, vol_now, sensitivity, block_pairs, book_order):
    rescaled = (returns.astype(jnp.float32) * vol_now[None, :] / vol_hist).astype(jnp.bfloat16)
    groups = lax.axis_size("blk")
    column = lax.axis_index("blk")
    block_size = sensitivity.shape[1]
    own_width = rescaled.shape[1] // groups
    gathered = lax.all_gather(rescaled, "blk", axis=0, tiled=True)
    own_shocks = lax.dynamic_slice_in_dim(gathered, column * own_width, own_width, 1)
    scen_rows = own_shocks.shape[0]
    local_blocks = own_shocks.reshape(scen_rows, own_width // block_size, block_size)
    factor_local = block_pairs[:, 0] - column * (own_width // block_size)
    picked = jnp.take(local_blocks, factor_local, axis=1)
    products = jnp.einsum("skc,kcd->ksd", picked, sensitivity, preferred_element_type=jnp.float32)
    book_blocks = book_order.shape[0]
    matches = book_order[None, :] == block_pairs[:, 1][:, None]
    position = jnp.sum(
        jnp.where(matches, jnp.arange(book_blocks, dtype=jnp.int32)[None, :], 0), axis=1
    )
    live_weight = block_pairs[:, 2].astype(jnp.float32)
    selector = jnp.where(
        jnp.arange(book_blocks, dtype=jnp.int32)[:, None] == position[None, :],
        live_weight[None, :],
        0.0,
    )
    partial_sum = jnp.einsum("bk,ksd->bsd", selector, products, precision=lax.Precision.HIGHEST)
    owned_books = lax.psum_scatter(partial_sum, "blk", scatter_dimension=0, tiled=True)
    profit_loss = owned_books.transpose(1, 0, 2).reshape(scen_rows, -1)
    squares = lax.psum(jnp.sum(profit_loss * profit_loss, axis=0), "scen")
    total_rows = scen_rows * lax.axis_size("scen")
    book_rms = jnp.sqrt(squares / total_rows + 1e-06)
    return (profit_loss, book_rms)


def solution(mesh):
    return jax.shard_map(
        shards,
        mesh=mesh,
        in_specs=(
            P(("scen", "blk"), None),
            P(("scen", "blk"), None),
            P(),
            P("blk", None, None),
            P("blk", None),
            P(),
        ),
        out_specs=(P("scen", "blk"), P("blk")),
        check_vma=False,
    )
```

profile of v0, /device:TPU:2, one launch (start us, length us, event | category | flops | bytes accessed | tf_op | source)
XLA Modules:
  0.0 306.9 jit_solution(5500297832278596794)
XLA Ops:
  7.2 0.0 all-gather.3.cloned.1.call-start
  7.2 1.9 convert_bitcast_fusion
  9.1 0.0 all-gather.3.cloned.1.call-update
  9.1 0.0 reduce-scatter.2.cloned.1.call-start
  9.2 0.7 and_reduce_fusion
  9.9 0.8 fusion.15
  10.7 0.8 select_reduce_fusion
  11.5 93.0 %all-gather.3.cloned.1.call-done = bf16[64,1,32768]{2,1,0:T(2,128)(2,1)} async-done(((bf16[1,1,32768]{2,1,0:T(2,128)(2,1)}), bf16[64,1,32768]{2,1,0:T(2,128)(2,1)}) %all-gather.3.cloned.1.call-update) | async-done | bytes 4194320 | tf_op jit(solution)/shard_map/all_gather | solution.py:13
  104.5 1.3 dynamic-slice_reduce_fusion
  105.8 3.0 gather_fusion
  108.8 7.0 %fusion.2 = f32[256,64,128]{2,1,0:T(8,128)S(1)} fusion(bf16[256,128,128]{2,1,0:T(8,128)(2,1)} %param.9, bf16[256,64,128]{2,1,0:T(8,128)(2,1)} %gather_fusion, pred[256]{0:T(512)(128)(4,1)S(1)} %get-tuple-element.2), kind=kOutput, calls=%fused_computation.3 | convolution fusion | flops 538968064 | bytes 20971776 | tf_op jit(solution)/shard_map/skc,kcd->ksd/dot_general | solution.py:19
  115.9 10.2 %fusion = f32[128,64,128]{2,0,1:T(8,128)S(1)} fusion(f32[256,64,128]{2,1,0:T(8,128)S(1)} %fusion.2, f32[256]{0:T(256)S(1)} %bitcast.32, s32[256]{0:T(256)S(1)} %select_reduce_fusion), kind=kOutput, calls=%fused_computation.1 | convolution fusion | flops 3221291008 | bytes 12584960 | tf_op jit(solution)/shard_map/bk,ksd->bsd/dot_general | solution.py:31
  126.1 4.4 %copy.18 = f32[128,64,128]{2,1,0:T(8,128)} copy(f32[128,64,128]{2,0,1:T(8,128)S(1)} %fusion) | data formatting | bytes 8388608 | tf_op jit(solution)/shard_map/bk,ksd->bsd/dot_general | solution.py:31
  130.4 0.0 reduce-scatter.2.cloned.1.call-update
  130.5 149.7 %reduce-scatter.2.cloned.1.call-done = f32[2,64,128]{2,1,0:T(8,128)} async-done(((f32[128,64,128]{2,1,0:T(8,128)}), f32[2,64,128]{2,1,0:T(8,128)}) %reduce-scatter.2.cloned.1.call-update) | async-done | bytes 65552 | tf_op jit(solution)/shard_map/reduce_scatter | solution.py:32
  280.2 0.9 fusion.9
  281.1 17.0 %psum.7 = f32[256]{0:T(256)S(1)} all-reduce(f32[256]{0:T(256)S(1)} %bitcast.29), channel_id=1, replica_groups=mesh['scen'=8,'blk'=64] {'scen'}, use_global_device_ids=true, to_apply=%region_3.4 | all-reduce | flops 256 | bytes 2048 | tf_op jit(solution)/shard_map/psum | solution.py:34
  298.0 0.6 add_sqrt_fusion
  298.6 1.5 copy_bitcast_fusion
  (2 shorter events, 0.0 us)
Async XLA Ops:
  7.2 97.4 %all-gather.3.cloned.1.call-start = ((), (), s32[]{:S(2)}) async-start(), calls=%async_computation.2 | async-start | bytes 8519680 | tf_op jit(solution)/shard_map/all_gather | solution.py:13
  9.1 271.0 %reduce-scatter.2.cloned.1.call-start = ((), (), s32[]{:S(2)}) async-start(), calls=%async_computation.1 | async-start | bytes 4259840 | tf_op jit(solution)/shard_map/reduce_scatter | solution.py:32
Sparse Core Ops, SparseCore 0:
  11.3 93.1 all-gather.2
  130.6 149.5 reduce-scatter.1
where the time goes:
time: 307 us
  waiting for transfers between devices  243 us (79%)
  matrix products  17.2 us (6%)
  blocking collectives  17 us (6%)
  between operations  14.1 us (5%)
  local copies, waits for them, and re-layouts  10.1 us (3%)
  other arithmetic  5.67 us (2%)
    reduce_scatter x1, waiting for transfers between devices, shards(): lax.psum_scatter(partial_sum, 'blk', scatter_dimension=0, tiled=True)  150 us
    all_gather x1, waiting for transfers between devices, shards(): gathered = lax.all_gather(rescaled, 'blk', axis=0, tiled=True)  93 us
    psum x1, blocking collectives, shards(): squares = lax.psum(jnp.sum(profit_loss * profit_loss, axis=0), 'scen')  17 us
    dot_general x1, matrix products, shards(): jnp.einsum('bk,ksd->bsd', selector, products, precision=lax.Precision.HIG...  10.2 us
    dot_general x1, matrix products, shards(): jnp.einsum('skc,kcd->ksd', picked, sensitivity, preferred_element_type=jn...  7.02 us
  transfers between devices with their start and end apart: 2, of which 2 were waited for; matrix products, arithmetic and copies ran while one was open for 1% of the time, Pallas kernels for 0%

commit v1 on v0

--- a/solution.py
+++ b/solution.py
@@ -10,7 +10,11 @@
     column = lax.axis_index("blk")
     block_size = sensitivity.shape[1]
     own_width = rescaled.shape[1] // groups
-    gathered = lax.all_gather(rescaled, "blk", axis=0, tiled=True)
+    size = lax.axis_size("blk")
+    repeats = [size if d == 0 else 1 for d in range(rescaled.ndim)]
+    gathered = lax.all_to_all(
+        jnp.tile(rescaled, repeats), "blk", split_axis=0, concat_axis=0, tiled=True
+    )
     own_shocks = lax.dynamic_slice_in_dim(gathered, column * own_width, own_width, 1)
     scen_rows = own_shocks.shape[0]
     local_blocks = own_shocks.reshape(scen_rows, own_width // block_size, block_size)

time: 307 us -> 382 us (1.24)
  local copies, waits for them, and re-layouts: 10.1 us -> 43.9 us
  other arithmetic: 5.67 us -> 29.9 us
  starting transfers between devices: 0.08 us -> 14.2 us
    all_to_all x0 -> x1, waiting for transfers between devices: none -> 95.8 us  [shards(): lax.all_to_all(jnp.tile(rescaled, repeats), 'blk', split_axis=0, concat_a...]
    all_gather x1 -> x0, waiting for transfers between devices: 93 us -> none  [shards(): gathered = lax.all_gather(rescaled, 'blk', axis=0, tiled=True)]
    unnamed x0 -> x6, local copies, waits for them, and re-layouts: none -> 27.6 us
    another operation x0 -> x1, other arithmetic: none -> 26.7 us  [shards(): jnp.tile(rescaled, repeats)]
    all_to_all x0 -> x1, starting transfers between devices: none -> 14.2 us  [shards(): lax.all_to_all(jnp.tile(rescaled, repeats), 'blk', split_axis=0, concat_a...]
    another operation x0 -> x2, local copies, waits for them, and re-layouts: none -> 6.13 us  [shards(): jnp.tile(rescaled, repeats)]
  transfers between devices with their start and end apart: 2 -> 2, of which waited for: 2 -> 2; matrix products, arithmetic and copies ran while one was open for 1% -> 0% of each run, Pallas kernels for 0% -> 0%
where the time goes in v1:
time: 382 us; the launch traced here: 381 us
  waiting for transfers between devices  244 us (64%)
  local copies, waits for them, and re-layouts  43.9 us (11%)
  other arithmetic  29.9 us (8%)
  matrix products  17.3 us (5%)
  blocking collectives  16.9 us (4%)
  starting transfers between devices  14.2 us (4%)
  between operations  14.1 us (4%)
    reduce_scatter x1, waiting for transfers between devices, shards(): lax.psum_scatter(partial_sum, 'blk', scatter_dimension=0, tiled=True)  148 us
    all_to_all x1, waiting for transfers between devices, shards(): lax.all_to_all(jnp.tile(rescaled, repeats), 'blk', split_axis=0, concat_a...  95.8 us
    unnamed x6, local copies, waits for them, and re-layouts  27.6 us
    another operation x1, other arithmetic, shards(): jnp.tile(rescaled, repeats)  26.7 us
    psum x1, blocking collectives, shards(): squares = lax.psum(jnp.sum(profit_loss * profit_loss, axis=0), 'scen')  16.9 us
    all_to_all x1, starting transfers between devices, shards(): lax.all_to_all(jnp.tile(rescaled, repeats), 'blk', split_axis=0, concat_a...  14.2 us
    dot_general x1, matrix products, shards(): jnp.einsum('bk,ksd->bsd', selector, products, precision=lax.Precision.HIG...  10.3 us
  transfers between devices with their start and end apart: 2, of which 2 were waited for; matrix products, arithmetic and copies ran while one was open for 0% of the time, Pallas kernels for 0%

profile of v1, /device:TPU:2, one launch (start us, length us, event | category | flops | bytes accessed | tf_op | source)
XLA Modules:
  0.0 380.6 jit_solution(13877792165904643910)
XLA Ops:
  7.2 1.5 convert_reduce_fusion
  8.7 5.6 %tile.2 = bf16[64,1,32768]{2,1,0:T(2,128)(2,1)} broadcast(bf16[32768]{0:T(1024)(128)(2,1)S(1)} %convert_reduce_fusion), dimensions={2} | broadcast | bytes 4259840 | tf_op jit(solution)/shard_map/tile | solution.py:16
  14.3 0.5 broadcast.37
  14.8 26.7 %reduce.7 = bf16[64,32768]{1,0:T(8,128)(2,1)} reduce(bf16[64,1,32768]{2,1,0:T(2,128)(2,1)} %tile.2, bf16[]{:T(256)} %broadcast.37), dimensions={1}, to_apply=%tile.2.reduce_sub_computation | reduce | bytes 8388610 | tf_op jit(solution)/shard_map/tile | solution.py:16
  41.5 7.8 %reshape.48 = bf16[64,2,16384]{2,1,0:T(2,128)(2,1)} reshape(bf16[64,32768]{1,0:T(8,128)(2,1)} %reduce.7) | data formatting | bytes 8388608
  49.3 0.0 copy-start
  49.3 14.2 %all-to-all-start = ((bf16[64,2,16384]{2,1,0:T(2,128)(2,1)}), bf16[64,2,16384]{2,1,0:T(2,128)(2,1)}, u32[]{:S(2)}, u32[]{:S(2)}) async-start(bf16[64,2,16384]{2,1,0:T(2,128)(2,1)} %reshape.48), calls=%async_computation | async-start | bytes 8388608 | tf_op jit(solution)/shard_map/all_to_all | solution.py:15
  63.5 0.0 reduce-scatter.2.cloned.1.call-start
  63.6 0.0 copy-done
  63.6 0.0 copy-done.1
  63.6 0.2 select_reduce_fusion
  63.8 95.8 %all-to-all-done = bf16[64,2,16384]{2,1,0:T(2,128)(2,1)} async-done(((bf16[64,2,16384]{2,1,0:T(2,128)(2,1)}), bf16[64,2,16384]{2,1,0:T(2,128)(2,1)}, u32[]{:S(2)}, u32[]{:S(2)}) %all-to-all-start) | async-done | bytes 4194336 | tf_op jit(solution)/shard_map/all_to_all | solution.py:15
  159.6 19.8 %reshape.49 = bf16[64,1,32768]{2,1,0:T(2,128)(2,1)} reshape(bf16[64,2,16384]{2,1,0:T(2,128)(2,1)} %all-to-all-done) | data formatting | bytes 8388608
  179.4 1.3 dynamic-slice_reduce_fusion
  180.7 3.0 gather_fusion
  183.7 7.0 %fusion.2 = f32[256,64,128]{2,1,0:T(8,128)S(1)} fusion(bf16[256,128,128]{2,1,0:T(8,128)(2,1)} %param.9, bf16[256,64,128]{2,1,0:T(8,128)(2,1)} %gather_fusion, pred[256]{0:T(512)(128)(4,1)S(1)} %get-tuple-element.2), kind=kOutput, calls=%fused_computation.3 | convolution fusion | flops 538968064 | bytes 20971776 | tf_op jit(solution)/shard_map/skc,kcd->ksd/dot_general | solution.py:23
  190.8 10.3 %fusion = f32[128,64,128]{2,0,1:T(8,128)S(1)} fusion(f32[256,64,128]{2,1,0:T(8,128)S(1)} %fusion.2, f32[256]{0:T(256)S(1)} %bitcast.30, s32[256]{0:T(256)S(1)} %select_reduce_fusion), kind=kOutput, calls=%fused_computation.1 | convolution fusion | flops 3221291008 | bytes 12584960 | tf_op jit(solution)/shard_map/bk,ksd->bsd/dot_general | solution.py:35
  201.0 4.4 %copy.18 = f32[128,64,128]{2,1,0:T(8,128)} copy(f32[128,64,128]{2,0,1:T(8,128)S(1)} %fusion) | data formatting | bytes 8388608 | tf_op jit(solution)/shard_map/bk,ksd->bsd/dot_general | solution.py:35
  205.4 0.0 reduce-scatter.2.cloned.1.call-update
  205.4 148.5 %reduce-scatter.2.cloned.1.call-done = f32[2,64,128]{2,1,0:T(8,128)} async-done(((f32[128,64,128]{2,1,0:T(8,128)}), f32[2,64,128]{2,1,0:T(8,128)}) %reduce-scatter.2.cloned.1.call-update) | async-done | bytes 65552 | tf_op jit(solution)/shard_map/reduce_scatter | solution.py:36
  353.9 0.9 fusion.9
  354.8 16.9 %psum.7 = f32[256]{0:T(256)S(1)} all-reduce(f32[256]{0:T(256)S(1)} %bitcast.27), channel_id=1, replica_groups=mesh['scen'=8,'blk'=64] {'scen'}, use_global_device_ids=true, to_apply=%region_3.4 | all-reduce | flops 256 | bytes 2048 | tf_op jit(solution)/shard_map/psum | solution.py:38
  371.7 0.6 add_sqrt_fusion
  372.2 1.5 copy_bitcast_fusion
  (5 shorter events, 0.1 us)
Async XLA Ops:
  49.3 14.3 %copy-start = (s32[256,3]{0,1:T(4,128)S(1)}, s32[256,3]{0,1:T(4,128)}, u32[]{:S(2)}) copy-start(s32[256,3]{0,1:T(4,128)} %param.10) | copy-start | bytes 9220
  49.3 14.3 %copy-start.1 = (s32[128]{0:T(128)S(1)}, s32[128]{0:T(128)}, u32[]{:S(2)}) copy-start(s32[128]{0:T(128)} %param.11) | copy-start | bytes 1540
  49.3 110.3 %all-to-all-start = ((bf16[64,2,16384]{2,1,0:T(2,128)(2,1)}), bf16[64,2,16384]{2,1,0:T(2,128)(2,1)}, u32[]{:S(2)}, u32[]{:S(2)}) async-start(bf16[64,2,16384]{2,1,0:T(2,128)(2,1)} %reshape.48), calls=%async_computation | async-start | bytes 8388608 | tf_op jit(solution)/shard_map/all_to_all | solution.py:15
  63.5 290.4 %reduce-scatter.2.cloned.1.call-start = ((), (), s32[]{:S(2)}) async-start(), calls=%async_computation.2 | async-start | bytes 4259840 | tf_op jit(solution)/shard_map/reduce_scatter | solution.py:36
Sparse Core Ops, SparseCore 0:
  205.5 148.3 reduce-scatter.1
